TPU v7x, 32 devices: a whole 2x2x4 slice. The times are simulated.
32 devices in a mesh: rows: 8 (over z, y), chan: 4 (over x, core).
Axes of the slice: x: 2, y: 2, z: 4, core: 2. Of those that a mesh axis runs over, the one named last changes fastest.
Arguments:
- radiances: float32 [16, 16384], P('chan', 'rows'), may hold values from -6 to 6
- band: int32 [16384, 1], P('rows'), may hold values from 0 to 7; in each aligned block of 2048 rows (0 to 2047, 2048 to 4095, ...) at most 512 rows name the same one
- row_in_band: int32 [16384], P('rows'), may hold values from 0 to 3
- column: int32 [16384], P('rows'), may hold values from 0 to 1439
Outputs:
- cell_count: int32 [32, 1440], P('rows')
- cell_mean: float32 [16, 32, 1440], P('chan', 'rows')
- cell_var: float32 [16, 32, 1440], P('chan', 'rows')
- cell_spread: float32 [32, 1440], P('rows')
- departure: float32 [16, 16384], P('chan', 'rows')
Inputs may be any that keep to these rules, and one draw needn't show every extreme that they name: Within each aligned block of 2048 observations (one scan-time shard) no band is named by more than 512 observations, and in some blocks one band is named by exactly 512.
All inputs are finite; a program needn't handle non-finite values.
Results may differ from a plain program's by a relative error of at most 0.0003.
Values sent between devices are 32-bit elements.
A program may use at most 64 MiB of HBM per device.

v0:
```python
import math

import jax
import jax.numpy as jnp
from jax import lax
from jax.sharding import PartitionSpec as P

CHAN = 16
COLS = 1440
ROWS_DEV = 4


def slot_ranks(dest, nrows):
    obs_dev = dest.shape[0]
    width = math.gcd(obs_dev, 128)
    nblock = obs_dev // width
    owners = jnp.arange(nrows, dtype=jnp.int32)
    hot = (dest[None, :] == owners[:, None]).astype(jnp.bfloat16).reshape(nrows, nblock, width)
    upper = (
        lax.broadcasted_iota(jnp.int32, (width, width), 0)
        <= lax.broadcasted_iota(jnp.int32, (width, width), 1)
    ).astype(jnp.bfloat16)
    inner = jnp.einsum("nbk,kj->nbj", hot, upper, preferred_element_type=jnp.float32)
    hot_float = hot.astype(jnp.float32)
    totals = jnp.sum(hot_float, axis=2)
    before = jnp.cumsum(totals, axis=1) - totals
    ranks = jnp.sum(hot_float * (inner + before[:, :, None]), axis=0).reshape(obs_dev) - 1.0
    return ranks.astype(jnp.int32)


def split_pair(values):
    high = lax.optimization_barrier(values.astype(jnp.bfloat16))
    low = (values - high.astype(jnp.float32)).astype(jnp.bfloat16)
    return (high, low)


def split_three(values):
    high = lax.optimization_barrier(values.astype(jnp.bfloat16))
    rest = values - high.astype(jnp.float32)
    middle = lax.optimization_barrier(rest.astype(jnp.bfloat16))
    low = (rest - middle.astype(jnp.float32)).astype(jnp.bfloat16)
    return (high, middle, low)


def grid_lookup(table, lat_index, col_index):
    fields, nlat, ncol = table.shape
    total = lat_index.shape[0]
    width = math.gcd(total, 2048)
    flat = table.reshape(fields * nlat, ncol)
    lat_iota = jnp.arange(nlat, dtype=jnp.int32)
    col_iota = jnp.arange(ncol, dtype=jnp.int32)

    def look_turn(turn, result):
        start = turn * width
        lat_part = lax.dynamic_slice_in_dim(lat_index, start, width, 0)
        col_part = lax.dynamic_slice_in_dim(col_index, start, width, 0)
        col_hot = (col_iota[:, None] == col_part[None, :]).astype(jnp.float32)
        picked = jnp.dot(
            flat, col_hot, precision=lax.Precision.HIGHEST, preferred_element_type=jnp.float32
        ).reshape(fields, nlat, width)
        lat_hot = (lat_iota[:, None] == lat_part[None, :]).astype(jnp.float32)
        found = jnp.sum(picked * lat_hot[None], axis=1)
        return lax.dynamic_update_slice_in_dim(result, found, start, 1)

    return lax.fori_loop(0, total // width, look_turn, jnp.zeros((fields, total), jnp.float32))


def body(radiances, band, row_in_band, column):
    nrows = lax.axis_size("rows")
    chan_dev, obs_dev = radiances.shape
    cap = 2 * obs_dev // nrows
    total_slots = nrows * cap
    dest = band[:, 0]
    slot = dest * cap + slot_ranks(dest, nrows)
    rad_high, rad_middle, rad_low = split_three(radiances)
    payload = jnp.concatenate(
        [
            rad_high,
            rad_middle,
            rad_low,
            row_in_band[None, :].astype(jnp.bfloat16),
            (column // 64)[None, :].astype(jnp.bfloat16),
            (column % 64)[None, :].astype(jnp.bfloat16),
            jnp.ones((1, obs_dev), jnp.bfloat16),
        ],
        axis=0,
    )
    nload = payload.shape[0]
    span = math.gcd(total_slots, 1024)
    slot_iota = jnp.arange(span, dtype=jnp.int32)

    def pack_turn(turn, buffer):
        start = turn * span
        hot = (slot[:, None] == (start + slot_iota)[None, :]).astype(jnp.bfloat16)
        placed_part = jnp.dot(payload, hot, preferred_element_type=jnp.float32)
        return lax.dynamic_update_slice_in_dim(buffer, placed_part, start, 1)

    placed = lax.fori_loop(
        0, total_slots // span, pack_turn, jnp.zeros((nload, total_slots), jnp.float32)
    )
    sent_values = (
        placed[0:chan_dev] + placed[chan_dev : 2 * chan_dev] + placed[2 * chan_dev : 3 * chan_dev]
    )
    base = 3 * chan_dev
    sent_cell = jnp.where(
        placed[base + 3] > 0.5,
        placed[base] * COLS + placed[base + 1] * 64.0 + placed[base + 2],
        -1.0,
    )
    packed = jnp.concatenate([sent_values, sent_cell[None, :]], axis=0).reshape(
        chan_dev + 1, nrows, cap
    )
    arrived = lax.all_to_all(packed, "rows", split_axis=1, concat_axis=1, tiled=True).reshape(
        chan_dev + 1, total_slots
    )
    values = arrived[:chan_dev]
    cell = arrived[chan_dev].astype(jnp.int32)
    lat_local = jnp.where(cell >= 0, cell // COLS, -1)
    col_local = jnp.where(cell >= 0, cell % COLS, -1)
    value_high, value_low = split_pair(values)
    square_high, square_low = split_pair(values * values)
    features = jnp.concatenate(
        [jnp.ones((1, total_slots), jnp.bfloat16), value_high, value_low, square_high, square_low],
        axis=0,
    )
    nfeat = features.shape[0]
    row_hot = (lat_local[None, :] == jnp.arange(ROWS_DEV, dtype=jnp.int32)[:, None]).astype(
        jnp.bfloat16
    )
    left = (features[:, None, :] * row_hot[None, :, :]).reshape(nfeat * ROWS_DEV, total_slots)
    block = math.gcd(total_slots, 2048)
    turns = total_slots // block
    columns_all = jnp.arange(COLS, dtype=jnp.int32)

    def accumulate(turn, acc):
        start = turn * block
        part = lax.dynamic_slice_in_dim(left, start, block, 1)
        picked = lax.dynamic_slice_in_dim(col_local, start, block, 0)
        col_hot = (picked[:, None] == columns_all[None, :]).astype(jnp.bfloat16)
        return acc + jnp.dot(part, col_hot, preferred_element_type=jnp.float32)

    sums = lax.fori_loop(0, turns, accumulate, jnp.zeros((nfeat * ROWS_DEV, COLS), jnp.float32))
    sums = sums.reshape(nfeat, ROWS_DEV, COLS)
    count = sums[0]
    first = sums[1 : 1 + chan_dev] + sums[1 + chan_dev : 1 + 2 * chan_dev]
    second = sums[1 + 2 * chan_dev : 1 + 3 * chan_dev] + sums[1 + 3 * chan_dev :]
    denom = jnp.maximum(count, 1.0)[None]
    mean = first / denom
    var = jnp.maximum(second / denom - mean * mean, 0.0)
    spread = lax.psum(jnp.sum(var, axis=0), "chan")
    scale = lax.rsqrt(1.0 + spread / CHAN)
    fields = grid_lookup(jnp.concatenate([mean, scale[None]], axis=0), lat_local, col_local)
    shifted = (values - fields[:chan_dev]) * fields[chan_dev][None, :]
    returned = lax.all_to_all(
        shifted.reshape(chan_dev, nrows, cap), "rows", split_axis=1, concat_axis=1, tiled=True
    )
    returned_flat = returned.reshape(chan_dev, total_slots)

    def unplace(turn, result):
        start = turn * span
        hot = (slot[:, None] == (start + slot_iota)[None, :]).astype(jnp.float32)
        part = lax.dynamic_slice_in_dim(returned_flat, start, span, 1)
        return result + lax.dot_general(
            part,
            hot,
            (((1,), (1,)), ((), ())),
            precision=lax.Precision.HIGHEST,
            preferred_element_type=jnp.float32,
        )

    departure = lax.fori_loop(
        0, total_slots // span, unplace, jnp.zeros((chan_dev, obs_dev), jnp.float32)
    )
    return (count.astype(jnp.int32), mean, var, spread, departure)


def solution(mesh):
    in_specs = (P("chan", "rows"), P("rows", None), P("rows"), P("rows"))
    out_specs = (
        P("rows", None),
        P("chan", "rows", None),
        P("chan", "rows", None),
        P("rows", None),
        P("chan", "rows"),
    )
    return jax.shard_map(body, mesh=mesh, in_specs=in_specs, out_specs=out_specs, check_vma=False)
```

profile of v0, /device:TPU:0, one launch (start us, length us, event | category | flops | bytes accessed | tf_op | source)
XLA Modules:
  0.0 82.0 jit_solution(14672771929657307120)
XLA Ops:
  0.6 0.8 convert_element_type.110
  1.4 0.8 fusion.46
  2.2 0.8 subtract_convert_fusion.2
  2.9 0.7 fusion.50
  3.7 0.7 convert_element_type.115
  4.4 0.7 broadcast_multiply_fusion.1
  5.1 0.8 convert_reduce_fusion
  5.9 0.2 reduce_window_sum.11
  6.1 0.9 %fusion.39 = f32[16,128]{1,0:T(8,128)S(1)} fusion(f32[8,16]{1,0:T(8,128)S(1)} %sub.41, s32[16,128]{1,0:T(8,128)} %bitcast.49), kind=kOutput, calls=%fused_computation.36 | convolution fusion | flops 4323328 | bytes 16896 | tf_op jit(solution)/shard_map/nbk,kj->nbj/dot_general | solution.py:23
  7.0 0.1 concatenate.17
  7.2 5.7 %while.56 = (s32[]{:T(128)}, f32[16,4096]{1,0:T(8,128)S(1)}, s32[2048]{0:T(1024)S(1)}, bf16[16,2048]{1,0:T(8,128)(2,1)S(1)}, s32[]{:T(128)}, /*index=5*/s32[]{:T(128)}, s32[]{:T(128)}, s32[]{:T(128)}) while((s32[]{:T(128)}, f32[16,4096]{1,0:T(8,128)S(1)}, s32[2048]{0:T(1024)S(1)}, bf16[16,2048]{1,0:T(8,128)(2,1)S(1)}, s32[]{:T(128)}, ...), condition=%wide.region_4.5_spmd.clone, body=%wide.region_3.4_spmd.clone.sunk | while | flops 69207048 | bytes 147595 | solution.py:98
  7.2 1.4 %fusion.70 = f32[16,4096]{1,0:T(8,128)S(1)} fusion(f32[16,4096]{1,0:T(8,128)S(1)} %get-tuple-element.638, s32[]{:T(128)S(6)} %select_n.104, bf16[16,2048]{1,0:T(8,128)(2,1)S(1)} %get-tuple-element.648, s32[1024]{0:T(1024)S(1)} %iota_add_fusion.4, s32[2048]{0:T(1024)S(1)} %get-tuple-element.647), kind=kOutput, calls=%fused_computation.10.clone.1 | convolution fusion | flops 69206016 | bytes 143364 | tf_op jit(solution)/shard_map/while/body/eval_jaxpr/dot_general | solution.py:95
  8.6 1.4 %fusion.70 = f32[16,4096]{1,0:T(8,128)S(1)} fusion(f32[16,4096]{1,0:T(8,128)S(1)} %get-tuple-element.638, s32[]{:T(128)S(6)} %select_n.104, bf16[16,2048]{1,0:T(8,128)(2,1)S(1)} %get-tuple-element.648, s32[1024]{0:T(1024)S(1)} %iota_add_fusion.4, s32[2048]{0:T(1024)S(1)} %get-tuple-element.647), kind=kOutput, calls=%fused_computation.10.clone.1 | convolution fusion | flops 69206016 | bytes 143364 | tf_op jit(solution)/shard_map/while/body/eval_jaxpr/dot_general | solution.py:95
  10.0 1.4 %fusion.70 = f32[16,4096]{1,0:T(8,128)S(1)} fusion(f32[16,4096]{1,0:T(8,128)S(1)} %get-tuple-element.638, s32[]{:T(128)S(6)} %select_n.104, bf16[16,2048]{1,0:T(8,128)(2,1)S(1)} %get-tuple-element.648, s32[1024]{0:T(1024)S(1)} %iota_add_fusion.4, s32[2048]{0:T(1024)S(1)} %get-tuple-element.647), kind=kOutput, calls=%fused_computation.10.clone.1 | convolution fusion | flops 69206016 | bytes 143364 | tf_op jit(solution)/shard_map/while/body/eval_jaxpr/dot_general | solution.py:95
  11.4 1.4 %fusion.70 = f32[16,4096]{1,0:T(8,128)S(1)} fusion(f32[16,4096]{1,0:T(8,128)S(1)} %get-tuple-element.638, s32[]{:T(128)S(6)} %select_n.104, bf16[16,2048]{1,0:T(8,128)(2,1)S(1)} %get-tuple-element.648, s32[1024]{0:T(1024)S(1)} %iota_add_fusion.4, s32[2048]{0:T(1024)S(1)} %get-tuple-element.647), kind=kOutput, calls=%fused_computation.10.clone.1 | convolution fusion | flops 69206016 | bytes 143364 | tf_op jit(solution)/shard_map/while/body/eval_jaxpr/dot_general | solution.py:95
  12.9 0.1 compare_select_fusion
  12.9 0.7 pad_maximum_fusion
  13.6 7.3 %all-to-all-start = ((f32[5,8,512]{2,0,1:T(8,128)}), f32[5,8,512]{2,0,1:T(8,128)S(1)}, u32[]{:S(2)}, u32[]{:S(2)}) async-start(f32[5,8,512]{2,0,1:T(8,128)} %pad_maximum_fusion), calls=%async_computation | async-start | bytes 262144 | tf_op jit(solution)/shard_map/all_to_all | solution.py:113
  20.9 7.3 %all-to-all-done = f32[5,8,512]{2,0,1:T(8,128)S(1)} async-done(((f32[5,8,512]{2,0,1:T(8,128)}), f32[5,8,512]{2,0,1:T(8,128)S(1)}, u32[]{:S(2)}, u32[]{:S(2)}) %all-to-all-start) | async-done | bytes 81952 | tf_op jit(solution)/shard_map/all_to_all | solution.py:113
  28.3 0.1 compare_reduce_fusion
  28.5 0.1 broadcast_remainder_fusion
  28.7 0.5 concatenate.21
  29.2 0.3 broadcast_multiply_fusion
  29.5 0.1 mul.121
  29.6 5.4 %while.58 = (s32[]{:T(128)}, f32[68,1440]{1,0:T(8,128)S(1)}, bf16[68,4096]{1,0:T(8,128)(2,1)S(1)}, s32[4096]{0:T(1024)S(1)}, s32[]{:T(128)}, /*index=5*/s32[]{:T(128)}, s32[]{:T(128)}, s32[]{:T(128)}) while((s32[]{:T(128)}, f32[68,1440]{1,0:T(8,128)S(1)}, bf16[68,4096]{1,0:T(8,128)(2,1)S(1)}, s32[4096]{0:T(1024)S(1)}, s32[]{:T(128)}, ...), condition=%wide.region_6.7_spmd.clone, body=%wide.region_5.6_spmd.clone.sunk | while | flops 404225280 | bytes 1153685 | solution.py:142
  29.6 2.7 %fusion.75 = f32[68,1440]{1,0:T(8,128)S(1)} fusion(s32[2048]{0:T(1024)S(1)} %dynamic_slice.52, f32[68,1440]{1,0:T(8,128)S(1)} %get-tuple-element.662, bf16[68,4096]{1,0:T(8,128)(2,1)S(1)} %get-tuple-element.671, s32[]{:T(128)S(6)} %select_n.106, pred[]{:T(512)S(6)} %compare.9), kind=kOutput, calls=%fused_computation.23.clone.1 | convolution fusion | flops 404225280 | bytes 1137157 | tf_op jit(solution)/shard_map/while/body/eval_jaxpr/dot_general | solution.py:140
  32.3 2.7 %fusion.75 = f32[68,1440]{1,0:T(8,128)S(1)} fusion(s32[2048]{0:T(1024)S(1)} %dynamic_slice.52, f32[68,1440]{1,0:T(8,128)S(1)} %get-tuple-element.662, bf16[68,4096]{1,0:T(8,128)(2,1)S(1)} %get-tuple-element.671, s32[]{:T(128)S(6)} %select_n.106, pred[]{:T(512)S(6)} %compare.9), kind=kOutput, calls=%fused_computation.23.clone.1 | convolution fusion | flops 404225280 | bytes 1137157 | tf_op jit(solution)/shard_map/while/body/eval_jaxpr/dot_general | solution.py:140
  35.1 0.6 slice_maximum_fusion
  35.7 0.7 fusion.53
  36.5 10.3 %psum.7 = f32[4,1440]{1,0:T(4,128)S(1)} all-reduce(f32[4,1440]{1,0:T(4,128)S(1)} %get-tuple-element.508), channel_id=1, replica_groups=mesh['rows'=8,'chan'=4] {'chan'}, use_global_device_ids=true, to_apply=%region_8.9 | all-reduce | flops 5760 | bytes 46080 | tf_op jit(solution)/shard_map/psum | solution.py:150
  46.9 0.5 copy-done.1
  47.3 8.0 %while.57 = (s32[]{:T(128)}, f32[5,4096]{1,0:T(8,128)S(1)}, s32[4096]{0:T(1024)S(1)}, f32[20,1440]{1,0:T(8,128)S(1)}, s32[4096]{0:T(1024)S(1)}, /*index=5*/s32[]{:T(128)}, s32[]{:T(128)}, s32[]{:T(128)}, s32[]{:T(128)}) while((s32[]{:T(128)}, f32[5,4096]{1,0:T(8,128)S(1)}, s32[4096]{0:T(1024)S(1)}, f32[20,1440]{1,0:T(8,128)S(1)}, ...), condition=%wide.region_11.12_spmd.clone, body=%wide.region_9.11_spmd.clone.sunk | while | flops 710825984 | bytes 1057431 | solution.py:65
  47.3 3.7 %fusion.72 = f32[20,2048]{1,0:T(8,128)S(1)} fusion(f32[20,1440]{1,0:T(8,128)S(1)} %get-tuple-element.698, s32[2048]{0:T(1024)S(1)} %dynamic_slice.49), kind=kOutput, calls=%fused_computation.15.clone.1 | convolution fusion | flops 710737920 | bytes 287232 | tf_op jit(solution)/shard_map/while/body/eval_jaxpr/dot_general | solution.py:58
  51.1 0.1 reshape.182
  51.2 0.1 multiply_reduce_fusion.2
  51.3 3.7 %fusion.72 = f32[20,2048]{1,0:T(8,128)S(1)} fusion(f32[20,1440]{1,0:T(8,128)S(1)} %get-tuple-element.698, s32[2048]{0:T(1024)S(1)} %dynamic_slice.49), kind=kOutput, calls=%fused_computation.15.clone.1 | convolution fusion | flops 710737920 | bytes 287232 | tf_op jit(solution)/shard_map/while/body/eval_jaxpr/dot_general | solution.py:58
  55.1 0.1 reshape.182
  55.2 0.1 multiply_reduce_fusion.2
  55.3 0.6 subtract_multiply_fusion
  56.0 3.3 %all-to-all-start.1 = ((f32[4,8,512]{2,0,1:T(4,128)}), f32[4,8,512]{2,0,1:T(4,128)S(1)}, u32[]{:S(2)}, u32[]{:S(2)}) async-start(f32[4,8,512]{2,0,1:T(4,128)} %bitcast.11), calls=%async_computation.1 | async-start | bytes 131072 | tf_op jit(solution)/shard_map/all_to_all | solution.py:154
  59.4 6.8 %all-to-all-done.1 = f32[4,8,512]{2,0,1:T(4,128)S(1)} async-done(((f32[4,8,512]{2,0,1:T(4,128)}), f32[4,8,512]{2,0,1:T(4,128)S(1)}, u32[]{:S(2)}, u32[]{:S(2)}) %all-to-all-start.1) | async-done | bytes 65568 | tf_op jit(solution)/shard_map/all_to_all | solution.py:154
  66.2 15.2 %while.59 = (s32[]{:T(128)}, f32[4,2048]{1,0:T(4,128)S(1)}, f32[4,4096]{1,0:T(4,128)S(1)}, s32[2048]{0:T(1024)S(1)}, s32[]{:T(128)}, /*index=5*/s32[]{:T(128)}, s32[]{:T(128)}, s32[]{:T(128)}) while((s32[]{:T(128)}, f32[4,2048]{1,0:T(4,128)S(1)}, f32[4,4096]{1,0:T(4,128)S(1)}, s32[2048]{0:T(1024)S(1)}, s32[]{:T(128)}, ...), condition=%wide.region_13.14_spmd.clone, body=%wide.region_12.13_spmd.clone.sunk | while | flops 102777864 | bytes 98453 | solution.py:171
  66.2 3.8 %fusion.78 = f32[4,2048]{1,0:T(4,128)S(1)} fusion(s32[1024]{0:T(1024)S(1)} %iota_add_fusion.5, s32[2048]{0:T(1024)S(1)} %get-tuple-element.723, f32[4,2048]{1,0:T(4,128)S(1)} %get-tuple-element.713, f32[4,4096]{1,0:T(4,128)S(1)} %get-tuple-element.722, s32[]{:T(128)S(6)} %select_n.107, pred[]{:T(512)S(6)} %compare.10), kind=kOutput, calls=%fused_computation.30.clone.1 | convolution fusion | flops 102776832 | bytes 94213 | tf_op jit(solution)/shard_map/while/body/eval_jaxpr/dot_general | solution.py:163
  70.0 3.8 %fusion.78 = f32[4,2048]{1,0:T(4,128)S(1)} fusion(s32[1024]{0:T(1024)S(1)} %iota_add_fusion.5, s32[2048]{0:T(1024)S(1)} %get-tuple-element.723, f32[4,2048]{1,0:T(4,128)S(1)} %get-tuple-element.713, f32[4,4096]{1,0:T(4,128)S(1)} %get-tuple-element.722, s32[]{:T(128)S(6)} %select_n.107, pred[]{:T(512)S(6)} %compare.10), kind=kOutput, calls=%fused_computation.30.clone.1 | convolution fusion | flops 102776832 | bytes 94213 | tf_op jit(solution)/shard_map/while/body/eval_jaxpr/dot_general | solution.py:163
  73.8 3.8 %fusion.78 = f32[4,2048]{1,0:T(4,128)S(1)} fusion(s32[1024]{0:T(1024)S(1)} %iota_add_fusion.5, s32[2048]{0:T(1024)S(1)} %get-tuple-element.723, f32[4,2048]{1,0:T(4,128)S(1)} %get-tuple-element.713, f32[4,4096]{1,0:T(4,128)S(1)} %get-tuple-element.722, s32[]{:T(128)S(6)} %select_n.107, pred[]{:T(512)S(6)} %compare.10), kind=kOutput, calls=%fused_computation.30.clone.1 | convolution fusion | flops 102776832 | bytes 94213 | tf_op jit(solution)/shard_map/while/body/eval_jaxpr/dot_general | solution.py:163
  77.6 3.8 %fusion.78 = f32[4,2048]{1,0:T(4,128)S(1)} fusion(s32[1024]{0:T(1024)S(1)} %iota_add_fusion.5, s32[2048]{0:T(1024)S(1)} %get-tuple-element.723, f32[4,2048]{1,0:T(4,128)S(1)} %get-tuple-element.713, f32[4,4096]{1,0:T(4,128)S(1)} %get-tuple-element.722, s32[]{:T(128)S(6)} %select_n.107, pred[]{:T(512)S(6)} %compare.10), kind=kOutput, calls=%fused_computation.30.clone.1 | convolution fusion | flops 102776832 | bytes 94213 | tf_op jit(solution)/shard_map/while/body/eval_jaxpr/dot_general | solution.py:163
  81.4 0.0 copy-start.2
  81.4 0.6 copy-done.2
  (48 shorter events, 0.6 us)
Async XLA Ops:
  13.6 14.7 %all-to-all-start = ((f32[5,8,512]{2,0,1:T(8,128)}), f32[5,8,512]{2,0,1:T(8,128)S(1)}, u32[]{:S(2)}, u32[]{:S(2)}) async-start(f32[5,8,512]{2,0,1:T(8,128)} %pad_maximum_fusion), calls=%async_computation | async-start | bytes 262144 | tf_op jit(solution)/shard_map/all_to_all | solution.py:113
  36.4 10.4 %copy-start = (f32[4,4,1440]{2,1,0:T(4,128)}, f32[4,4,1440]{2,1,0:T(4,128)S(1)}, u32[]{:S(2)}) copy-start(f32[4,4,1440]{2,1,0:T(4,128)S(1)} %get-tuple-element.510) | copy-start | bytes 276484
  46.7 0.6 copy-start.1
  56.0 10.2 %all-to-all-start.1 = ((f32[4,8,512]{2,0,1:T(4,128)}), f32[4,8,512]{2,0,1:T(4,128)S(1)}, u32[]{:S(2)}, u32[]{:S(2)}) async-start(f32[4,8,512]{2,0,1:T(4,128)} %bitcast.11), calls=%async_computation.1 | async-start | bytes 131072 | tf_op jit(solution)/shard_map/all_to_all | solution.py:154
  81.4 0.6 copy-start.2
where the time goes:
time: 82.7 us; the launch traced here: 82 us
  matrix products  34.5 us (42%)
  waiting for transfers between devices  14.2 us (17%)
  starting transfers between devices  10.7 us (13%)
  blocking collectives  10.3 us (12%)
  other arithmetic  9.1 us (11%)
  local copies, waits for them, and re-layouts  2.18 us (3%)
  between operations  0.93 us (1%)
    dot_general x4, matrix products, unplace(): lax.dot_general(part, hot, (((1,), (1,)), ((), ())), precision=lax.Precis...  15.1 us
    psum x1, blocking collectives, body(): spread = lax.psum(jnp.sum(var, axis=0), 'chan')  10.3 us
    dot_general x2, matrix products, look_turn(): jnp.dot(flat, col_hot, precision=lax.Precision.HIGHEST, preferred_element...  7.49 us
    all_to_all x1, waiting for transfers between devices, body(): lax.all_to_all(packed, 'rows', split_axis=1, concat_axis=1, tiled=True)  7.34 us
    all_to_all x1, starting transfers between devices, body(): lax.all_to_all(packed, 'rows', split_axis=1, concat_axis=1, tiled=True)  7.31 us
    all_to_all x1, waiting for transfers between devices, body(): lax.all_to_all(shifted.reshape(chan_dev, nrows, cap), 'rows', split_axis=...  6.83 us
    dot_general x4, matrix products, pack_turn(): placed_part = jnp.dot(payload, hot, preferred_element_type=jnp.float32)  5.63 us
    dot_general x2, matrix products, accumulate(): return acc + jnp.dot(part, col_hot, preferred_element_type=jnp.float32)  5.3 us
  transfers between devices with their start and end apart: 2, of which 2 were waited for; matrix products, arithmetic and copies ran while one was open for 0% of the time, Pallas kernels for 0%

commit v1 on v0

v1 whole, which is shorter than its diff:
```python
import functools

import jax
import jax.numpy as jnp
from jax import lax
from jax.experimental import pallas as pl
from jax.experimental.pallas import tpu as pltpu
from jax.sharding import PartitionSpec as P

CHAN = 16
COLS = 1440
ROWS_DEV = 4
LOW = 256
BLOCKS = -(-COLS // LOW)
QS = BLOCKS * ROWS_DEV
F32 = jnp.float32
BF16 = jnp.bfloat16
MESH = pl.DeviceIdType.MESH
NT = (((1,), (1,)), ((), ()))
NN = (((1,), (0,)), ((), ()))


def iota(shape, axis):
    return lax.broadcasted_iota(jnp.int32, shape, axis)


def onehot(mask):
    return jnp.where(mask, 1.0, 0.0)


def two(values):
    high = values.astype(BF16).astype(F32)
    return high, values - high


def dot(a, b, dims):
    return lax.dot_general(a, b, dims, preferred_element_type=F32)


def rank_of(dest, nrows):
    obs = dest.shape[1]
    nblock = obs // 128
    hot = onehot(iota((nrows, obs), 0) == dest)
    stacked = jnp.concatenate([hot[:, b * 128 : (b + 1) * 128] for b in range(nblock)], axis=0)
    stacked_b = stacked.astype(BF16)
    size = nblock * nrows
    upper = onehot(iota((128, 128), 0) <= iota((128, 128), 1)).astype(BF16)
    inner = dot(stacked_b, upper, NN)
    r, c = iota((size, size), 0), iota((size, size), 1)
    earlier = onehot((c < r) & (lax.rem(r - c + size, nrows) == 0)).astype(BF16)
    before = jnp.sum(dot(earlier, stacked_b, NN), axis=1, keepdims=True)
    ranks = stacked * (inner + before)
    rows = [
        jnp.sum(ranks[b * nrows : (b + 1) * nrows], axis=0, keepdims=True) for b in range(nblock)
    ]
    return (jnp.concatenate(rows, axis=1) - 1.0).astype(jnp.int32)


def spill(out, values):
    for j in range(BLOCKS):
        start = j * LOW
        width = min(LOW, COLS - start)
        out[:, start : start + width] = values[j * ROWS_DEV : (j + 1) * ROWS_DEV, :width].astype(
            out.dtype
        )


def kernel(
    nrows,
    nchan,
    rad_ref,
    band_ref,
    rib_ref,
    col_ref,
    cnt_out,
    mean_out,
    var_out,
    spr_out,
    dep_out,
    rank_hot,
    col_hot,
    q_hot,
    acc,
    send_v,
    send_c,
    recv_v,
    recv_c,
    parts,
    back_s,
    back_r,
    sv,
    rv,
    sc,
    rc,
    sp,
    rp,
    sb,
    rb,
):
    me = lax.axis_index("rows")
    mc = lax.axis_index("chan")
    fields, obs = rad_ref.shape
    cap = rank_hot.shape[0]

    barrier = pltpu.get_barrier_semaphore()
    for d in range(1, nrows):
        pl.semaphore_signal(
            barrier, inc=1, device_id={"rows": lax.rem(me + d, nrows)}, device_id_type=MESH
        )
    for d in range(1, nchan):
        pl.semaphore_signal(
            barrier, inc=1, device_id={"chan": lax.rem(mc + d, nchan)}, device_id_type=MESH
        )

    dest = band_ref[...]
    rank = rank_of(dest, nrows)
    rank_hot[...] = onehot(iota((cap, obs), 0) == rank).astype(BF16)
    rad = rad_ref[...]
    high, rest = two(rad)
    middle, low = two(rest)
    col = col_ref[...]
    code = (col // LOW) * ROWS_DEV + rib_ref[...] + 1
    pad = -(3 * fields + 2) % 8
    group = 3 * fields + 2 + pad
    payload = jnp.concatenate(
        [high, middle, low, code.astype(F32), (col % LOW).astype(F32), jnp.zeros((pad, obs), F32)],
        axis=0,
    )
    left = jnp.concatenate(
        [jnp.where(dest == lax.rem(me + d, nrows), payload, 0.0) for d in range(nrows)], axis=0
    ).astype(BF16)
    placed = dot(left, rank_hot[...], NT)
    pl.semaphore_wait(barrier, nrows - 1 + nchan - 1)

    out_copies = []
    for d in list(range(1, nrows)) + [0]:
        part = placed[d * group : (d + 1) * group]
        values = (part[:fields] + part[fields : 2 * fields]) + part[2 * fields : 3 * fields]
        cells = part[3 * fields : 3 * fields + 1] * LOW + part[3 * fields + 1 : 3 * fields + 2]
        if d == 0:
            recv_v[0] = values
            recv_c[0] = cells
            continue
        send_v[d] = values
        send_c[d] = cells
        to = {"rows": lax.rem(me + d, nrows)}
        for src, dst, s, r in ((send_v, recv_v, sv, rv), (send_c, recv_c, sc, rc)):
            copy = pltpu.make_async_remote_copy(
                src_ref=src.at[d],
                dst_ref=dst.at[d],
                send_sem=s.at[d],
                recv_sem=r.at[d],
                device_id=to,
                device_id_type=MESH,
            )
            copy.start()
            out_copies.append(copy)

    for d in range(nrows):
        if d > 0:
            out_copies[2 * d - 2].wait_recv()
            out_copies[2 * d - 1].wait_recv()
        values = recv_v[d]
        cells = recv_c[d].astype(jnp.int32)
        cols_t = onehot(iota((LOW, cap), 0) == (cells & (LOW - 1))).astype(BF16)
        col_hot[d] = cols_t
        quads = onehot(iota((QS, cap), 0) == (cells // LOW) - 1)
        q_hot[d] = quads
        features = two(values) + two(values * values)
        rows = [quads] + [quads * x[f : f + 1] for x in features for f in range(fields)]
        sums = dot(jnp.concatenate(rows, axis=0).astype(BF16), cols_t, NT)
        if d == 0:
            acc[...] = sums
        else:
            acc[...] += sums

    count = acc[0:QS]
    inverse = 1.0 / jnp.maximum(count, 1.0)
    means, variances = [], []
    for f in range(fields):

        def total(k):
            at = (1 + k * fields + f) * QS
            after = at + fields * QS
            return acc[at : at + QS] + acc[after : after + QS]

        mean = total(0) * inverse
        means.append(mean)
        variances.append(jnp.maximum(total(2) * inverse - mean * mean, 0.0))
    partial = variances[0]
    for f in range(1, fields):
        partial = partial + variances[f]
    parts[mc] = partial
    part_copies = []
    for d in range(1, nchan):
        copy = pltpu.make_async_remote_copy(
            src_ref=parts.at[mc],
            dst_ref=parts.at[mc],
            send_sem=sp.at[d],
            recv_sem=rp.at[d],
            device_id={"chan": lax.rem(mc + d, nchan)},
            device_id_type=MESH,
        )
        copy.start()
        part_copies.append(copy)

    spill(cnt_out, count)
    for f in range(fields):
        spill(mean_out.at[f], means[f])
        spill(var_out.at[f], variances[f])
    split = [two(mean) for mean in means]
    table = jnp.concatenate([x[0] for x in split] + [x[1] for x in split], axis=0).astype(BF16)
    for d in range(nrows):
        picked = dot(table, col_hot[d], NN)
        quads = q_hot[d]
        found = []
        for f in range(fields):
            at = (fields + f) * QS
            both = picked[f * QS : (f + 1) * QS] + picked[at : at + QS]
            found.append(jnp.sum(both * quads, axis=0, keepdims=True))
        back_s[d] = recv_v[d] - jnp.concatenate(found, axis=0)

    for copy in part_copies:
        copy.wait_recv()
    spread = parts[0]
    for c in range(1, nchan):
        spread = spread + parts[c]
    scale = lax.rsqrt(1.0 + spread / CHAN)
    table = jnp.concatenate(two(scale), axis=0).astype(BF16)
    back_copies = []
    for d in list(range(1, nrows)) + [0]:
        picked = dot(table, col_hot[d], NN)
        found = jnp.sum((picked[:QS] + picked[QS:]) * q_hot[d], axis=0, keepdims=True)
        shifted = back_s[d] * found
        if d == 0:
            back_r[0] = shifted
            continue
        back_s[d] = shifted
        copy = pltpu.make_async_remote_copy(
            src_ref=back_s.at[d],
            dst_ref=back_r.at[d],
            send_sem=sb.at[d],
            recv_sem=rb.at[d],
            device_id={"rows": lax.rem(me + nrows - d, nrows)},
            device_id_type=MESH,
        )
        copy.start()
        back_copies.append(copy)
    spill(spr_out, spread)

    for copy in back_copies:
        copy.wait_recv()
    returned = jnp.concatenate([back_r[d] for d in range(nrows)], axis=0)
    size = nrows * fields
    both = dot(jnp.concatenate(two(returned), axis=0).astype(BF16), rank_hot[...], NN)
    merged = both[:size] + both[size:]
    per = max(1, 8 // fields)
    inside = jnp.zeros((per * fields, 1), jnp.int32)
    for j in range(1, per):
        inside = inside + (iota((per * fields, 1), 0) >= j * fields).astype(jnp.int32)
    result = None
    for p in range(nrows // per):
        owner = lax.rem(me + p * per + inside, nrows)
        block = merged[p * per * fields : (p + 1) * per * fields]
        term = jnp.where(dest == owner, block, 0.0)
        result = term if result is None else result + term
    final = result[:fields]
    for j in range(1, per):
        final = final + result[j * fields : (j + 1) * fields]
    dep_out[...] = final

    for copy in out_copies + part_copies + back_copies:
        copy.wait_send()


def body(radiances, band, row_in_band, column):
    nrows = lax.axis_size("rows")
    nchan = lax.axis_size("chan")
    fields, obs = radiances.shape
    cap = 2 * obs // nrows
    nfeat = 1 + 4 * fields
    vmem = pl.BlockSpec(memory_space=pltpu.VMEM)
    dma = pltpu.SemaphoreType.DMA
    return pl.pallas_call(
        functools.partial(kernel, nrows, nchan),
        out_shape=(
            jax.ShapeDtypeStruct((ROWS_DEV, COLS), jnp.int32),
            jax.ShapeDtypeStruct((fields, ROWS_DEV, COLS), F32),
            jax.ShapeDtypeStruct((fields, ROWS_DEV, COLS), F32),
            jax.ShapeDtypeStruct((ROWS_DEV, COLS), F32),
            jax.ShapeDtypeStruct((fields, obs), F32),
        ),
        in_specs=[vmem] * 4,
        out_specs=(vmem,) * 5,
        scratch_shapes=[
            pltpu.VMEM((cap, obs), BF16),
            pltpu.VMEM((nrows, LOW, cap), BF16),
            pltpu.VMEM((nrows, QS, cap), F32),
            pltpu.VMEM((nfeat * QS, LOW), F32),
            pltpu.VMEM((nrows, fields, cap), F32),
            pltpu.VMEM((nrows, 1, cap), F32),
            pltpu.VMEM((nrows, fields, cap), F32),
            pltpu.VMEM((nrows, 1, cap), F32),
            pltpu.VMEM((nchan, QS, LOW), F32),
            pltpu.VMEM((nrows, fields, cap), F32),
            pltpu.VMEM((nrows, fields, cap), F32),
            dma((nrows,)),
            dma((nrows,)),
            dma((nrows,)),
            dma((nrows,)),
            dma((nchan,)),
            dma((nchan,)),
            dma((nrows,)),
            dma((nrows,)),
        ],
        compiler_params=pltpu.CompilerParams(collective_id=0, has_side_effects=True),
    )(
        radiances,
        band.reshape(1, obs),
        row_in_band.reshape(1, obs),
        column.reshape(1, obs),
    )


def solution(mesh):
    in_specs = (P("chan", "rows"), P("rows", None), P("rows"), P("rows"))
    out_specs = (
        P("rows", None),
        P("chan", "rows", None),
        P("chan", "rows", None),
        P("rows", None),
        P("chan", "rows"),
    )
    return jax.shard_map(body, mesh=mesh, in_specs=in_specs, out_specs=out_specs, check_vma=False)
```

time: 82.7 us -> 27.8 us (0.34)
  matrix products: 34.5 us -> 0 us
  Pallas kernels: 0 us -> 21.7 us
  waiting for transfers between devices: 14.2 us -> 0 us
  starting transfers between devices: 10.7 us -> 0 us
  blocking collectives: 10.3 us -> 0 us
  other arithmetic: 9.1 us -> 0 us
  local copies, waits for them, and re-layouts: 2.18 us -> 5.04 us
    dot_general x13 -> x0, matrix products: 34.5 us -> none  [the longest x4 15.1 us: unplace(): lax.dot_general(part, hot, (((1,), (1,)), ((), ())), precision=lax.Precis...]
    pallas_call x0 -> x1, Pallas kernels: none -> 21.7 us  [body(): pl.pallas_call(functools.partial(kernel, nrows, nchan), out_shape=(jax.Sh...]
    all_to_all x2 -> x0, waiting for transfers between devices: 14.2 us -> none  [the longest x1 7.34 us: body(): lax.all_to_all(packed, 'rows', split_axis=1, concat_axis=1, tiled=True)]
    all_to_all x2 -> x0, starting transfers between devices: 10.7 us -> none  [the longest x1 7.31 us: body(): lax.all_to_all(packed, 'rows', split_axis=1, concat_axis=1, tiled=True)]
    psum x1 -> x0, blocking collectives: 10.3 us -> none  [body(): spread = lax.psum(jnp.sum(var, axis=0), 'chan')]
    unnamed x8 -> x11, local copies, waits for them, and re-layouts: 1.1 us -> 5.04 us
    convert_element_type x11 -> x0, other arithmetic: 3.82 us -> none  [the longest x1 0.78 us: split_three(): low = (rest - middle.astype(jnp.float32)).astype(jnp.bfloat16)]
    reduce_sum x4 -> x0, other arithmetic: 1.7 us -> none  [the longest x1 0.78 us: slot_ranks(): totals = jnp.sum(hot_float, axis=2)]
  transfers between devices with their start and end apart: 2 -> 0, of which waited for: 2 -> 0; matrix products, arithmetic and copies ran while one was open for 0% -> 0% of each run, Pallas kernels for 0% -> 0%
where the time goes in v1:
time: 27.8 us; the launch traced here: 27.4 us
  Pallas kernels  21.7 us (78%)
  local copies, waits for them, and re-layouts  5.04 us (18%)
  between operations  0.65 us (2%)
    pallas_call x1, Pallas kernels, body(): pl.pallas_call(functools.partial(kernel, nrows, nchan), out_shape=(jax.Sh...  21.7 us
    unnamed x11, local copies, waits for them, and re-layouts  5.04 us

profile of v1, /device:TPU:0, one launch (start us, length us, event | category | flops | bytes accessed | tf_op | source)
XLA Modules:
  0.0 27.4 jit_solution(2130035055556124795)
XLA Ops:
  0.6 21.7 %shard_map.83 = (s32[4,1440]{1,0:T(4,128)}, f32[4,4,1440]{2,1,0:T(4,128)}, f32[4,4,1440]{2,1,0:T(4,128)}, f32[4,1440]{1,0:T(4,128)}, f32[4,2048]{1,0:T(4,128)}) custom-call(f32[4,2048]{1,0:T(4,128)} %rad_ref.1, s32[1,2048]{1,0:T(1,128)} %bitcast.3, s32[1,2048]{1,0:T(1,128)} %bitcast.4, s32[1,2048]{1,0:T(1,128)} %bitcast.5), custom_call_target="tpu_custom_call" | custom-call | tf_op jit(solution)/shard_map/pallas_call | solution.py:284
  22.3 1.3 %copy.14 = s32[4,1440]{1,0:T(4,128)} copy(s32[4,1440]{1,0:T(4,128)} %get-tuple-element.10) | data formatting | bytes 46080
  23.7 0.0 copy-start
  23.7 1.6 %copy.15 = f32[4,4,1440]{2,1,0:T(4,128)} copy(f32[4,4,1440]{2,1,0:T(4,128)} %get-tuple-element.11) | data formatting | bytes 184320
  25.3 0.0 copy-done
  25.3 0.0 copy-start.2
  25.3 0.6 %copy.16 = f32[4,4,1440]{2,1,0:T(4,128)} copy(f32[4,4,1440]{2,1,0:T(4,128)S(1)} %copy-done) | data formatting | bytes 184320
  25.9 0.1 copy-done.2
  26.0 0.0 copy-start.1
  26.0 0.6 %copy.17 = f32[4,1440]{1,0:T(4,128)} copy(f32[4,1440]{1,0:T(4,128)S(1)} %copy-done.2) | data formatting | bytes 46080
  26.6 0.2 copy-done.1
  26.8 0.6 %copy.18 = f32[4,2048]{1,0:T(4,128)} copy(f32[4,2048]{1,0:T(4,128)S(1)} %copy-done.1) | data formatting | bytes 65536
Async XLA Ops:
  23.7 1.6 %copy-start = (f32[4,4,1440]{2,1,0:T(4,128)S(1)}, f32[4,4,1440]{2,1,0:T(4,128)}, u32[]{:S(2)}) copy-start(f32[4,4,1440]{2,1,0:T(4,128)} %get-tuple-element.12) | copy-start | bytes 276484
  25.3 0.7 %copy-start.2 = (f32[4,1440]{1,0:T(4,128)S(1)}, f32[4,1440]{1,0:T(4,128)}, u32[]{:S(2)}) copy-start(f32[4,1440]{1,0:T(4,128)} %get-tuple-element.13) | copy-start | bytes 69124
  26.0 0.8 %copy-start.1 = (f32[4,2048]{1,0:T(4,128)S(1)}, f32[4,2048]{1,0:T(4,128)}, u32[]{:S(2)}) copy-start(f32[4,2048]{1,0:T(4,128)} %get-tuple-element.14) | copy-start | bytes 98308

commit v2 on v1

--- a/solution.py
+++ b/solution.py
@@ -65,19 +65,45 @@
         )
 
 
+def unplace(me, nrows, fields, returned, rank_hot, dest):
+    size = nrows * fields
+    both = dot(jnp.concatenate(two(returned), axis=0).astype(BF16), rank_hot[...], NN)
+    merged = both[:size] + both[size:]
+    per = max(1, 8 // fields)
+    inside = jnp.zeros((per * fields, 1), jnp.int32)
+    for j in range(1, per):
+        inside = inside + (iota((per * fields, 1), 0) >= j * fields).astype(jnp.int32)
+    result = None
+    for p in range(nrows // per):
+        owner = lax.rem(me + p * per + inside, nrows)
+        block = merged[p * per * fields : (p + 1) * per * fields]
+        term = jnp.where(dest == owner, block, 0.0)
+        result = term if result is None else result + term
+    final = result[:fields]
+    for j in range(1, per):
+        final = final + result[j * fields : (j + 1) * fields]
+    return final
+
+
 def kernel(
     nrows,
     nchan,
+    rad_in,
+    band_in,
+    rib_in,
+    col_in,
+    cnt_out,
+    mean_out,
+    var_out,
+    spr_out,
+    diff_out,
+    scale_out,
+    rank_hot,
+    dest_out,
     rad_ref,
     band_ref,
     rib_ref,
     col_ref,
-    cnt_out,
-    mean_out,
-    var_out,
-    spr_out,
-    dep_out,
-    rank_hot,
     col_hot,
     q_hot,
     acc,
@@ -88,6 +114,9 @@
     parts,
     back_s,
     back_r,
+    scale_s,
+    scale_r,
+    ins,
     sv,
     rv,
     sc,
@@ -96,12 +125,22 @@
     rp,
     sb,
     rb,
+    ss,
+    rs,
 ):
     me = lax.axis_index("rows")
     mc = lax.axis_index("chan")
     fields, obs = rad_ref.shape
     cap = rank_hot.shape[0]
 
+    fetches = [
+        pltpu.make_async_copy(a, b, ins.at[i])
+        for i, (a, b) in enumerate(
+            ((band_in, band_ref), (rad_in, rad_ref), (rib_in, rib_ref), (col_in, col_ref))
+        )
+    ]
+    for fetch in fetches:
+        fetch.start()
     barrier = pltpu.get_barrier_semaphore()
     for d in range(1, nrows):
         pl.semaphore_signal(
@@ -112,9 +151,13 @@
             barrier, inc=1, device_id={"chan": lax.rem(mc + d, nchan)}, device_id_type=MESH
         )
 
+    fetches[0].wait()
     dest = band_ref[...]
+    dest_out[...] = dest
     rank = rank_of(dest, nrows)
     rank_hot[...] = onehot(iota((cap, obs), 0) == rank).astype(BF16)
+    for fetch in fetches[1:]:
+        fetch.wait()
     rad = rad_ref[...]
     high, rest = two(rad)
     middle, low = two(rest)
@@ -204,13 +247,10 @@
         copy.start()
         part_copies.append(copy)
 
-    spill(cnt_out, count)
-    for f in range(fields):
-        spill(mean_out.at[f], means[f])
-        spill(var_out.at[f], variances[f])
     split = [two(mean) for mean in means]
     table = jnp.concatenate([x[0] for x in split] + [x[1] for x in split], axis=0).astype(BF16)
-    for d in range(nrows):
+    back_copies = []
+    for d in list(range(1, nrows)) + [0]:
         picked = dot(table, col_hot[d], NN)
         quads = q_hot[d]
         found = []
@@ -218,7 +258,21 @@
             at = (fields + f) * QS
             both = picked[f * QS : (f + 1) * QS] + picked[at : at + QS]
             found.append(jnp.sum(both * quads, axis=0, keepdims=True))
-        back_s[d] = recv_v[d] - jnp.concatenate(found, axis=0)
+        diff = recv_v[d] - jnp.concatenate(found, axis=0)
+        if d == 0:
+            back_r[0] = diff
+            continue
+        back_s[d] = diff
+        copy = pltpu.make_async_remote_copy(
+            src_ref=back_s.at[d],
+            dst_ref=back_r.at[d],
+            send_sem=sb.at[d],
+            recv_sem=rb.at[d],
+            device_id={"rows": lax.rem(me + nrows - d, nrows)},
+            device_id_type=MESH,
+        )
+        copy.start()
+        back_copies.append(copy)
 
     for copy in part_copies:
         copy.wait_recv()
@@ -227,50 +281,71 @@
         spread = spread + parts[c]
     scale = lax.rsqrt(1.0 + spread / CHAN)
     table = jnp.concatenate(two(scale), axis=0).astype(BF16)
-    back_copies = []
+    scale_copies = []
     for d in list(range(1, nrows)) + [0]:
         picked = dot(table, col_hot[d], NN)
         found = jnp.sum((picked[:QS] + picked[QS:]) * q_hot[d], axis=0, keepdims=True)
-        shifted = back_s[d] * found
         if d == 0:
-            back_r[0] = shifted
+            scale_r[0] = found
             continue
-        back_s[d] = shifted
+        scale_s[d] = found
         copy = pltpu.make_async_remote_copy(
-            src_ref=back_s.at[d],
-            dst_ref=back_r.at[d],
-            send_sem=sb.at[d],
-            recv_sem=rb.at[d],
+            src_ref=scale_s.at[d],
+            dst_ref=scale_r.at[d],
+            send_sem=ss.at[d],
+            recv_sem=rs.at[d],
             device_id={"rows": lax.rem(me + nrows - d, nrows)},
             device_id_type=MESH,
         )
         copy.start()
-        back_copies.append(copy)
+        scale_copies.append(copy)
     spill(spr_out, spread)
+    spill(cnt_out, count)
+    for f in range(fields):
+        spill(mean_out.at[f], means[f])
+        spill(var_out.at[f], variances[f])
 
     for copy in back_copies:
         copy.wait_recv()
     returned = jnp.concatenate([back_r[d] for d in range(nrows)], axis=0)
-    size = nrows * fields
-    both = dot(jnp.concatenate(two(returned), axis=0).astype(BF16), rank_hot[...], NN)
-    merged = both[:size] + both[size:]
-    per = max(1, 8 // fields)
-    inside = jnp.zeros((per * fields, 1), jnp.int32)
-    for j in range(1, per):
-        inside = inside + (iota((per * fields, 1), 0) >= j * fields).astype(jnp.int32)
-    result = None
-    for p in range(nrows // per):
-        owner = lax.rem(me + p * per + inside, nrows)
-        block = merged[p * per * fields : (p + 1) * per * fields]
-        term = jnp.where(dest == owner, block, 0.0)
-        result = term if result is None else result + term
-    final = result[:fields]
-    for j in range(1, per):
-        final = final + result[j * fields : (j + 1) * fields]
-    dep_out[...] = final
-
-    for copy in out_copies + part_copies + back_copies:
+    diff_out[...] = unplace(me, nrows, fields, returned, rank_hot, dest)
+    for copy in scale_copies:
+        copy.wait_recv()
+    scale_out[...] = jnp.concatenate([scale_r[d] for d in range(nrows)], axis=0)
+
+    for copy in out_copies + part_copies + back_copies + scale_copies:
         copy.wait_send()
+
+
+def finish(
+    nrows,
+    cnt_ref,
+    mean_ref,
+    var_ref,
+    spr_ref,
+    diff_ref,
+    scale_ref,
+    rank_hot,
+    band_ref,
+    cnt_out,
+    mean_out,
+    var_out,
+    spr_out,
+    dep_out,
+    sems,
+):
+    pairs = ((mean_ref, mean_out), (var_ref, var_out), (cnt_ref, cnt_out), (spr_ref, spr_out))
+    copies = [pltpu.make_async_copy(a, b, sems.at[i]) for i, (a, b) in enumerate(pairs)]
+    for copy in copies:
+        copy.start()
+    me = lax.axis_index("rows")
+    both = dot(jnp.concatenate(two(scale_ref[...]), axis=0).astype(BF16), rank_hot[...], NN)
+    merged = both[:nrows] + both[nrows:]
+    owner = lax.rem(me + iota((nrows, 1), 0), nrows)
+    mine = jnp.where(band_ref[...] == owner, merged, 0.0)
+    dep_out[...] = diff_ref[...] * jnp.sum(mine, axis=0, keepdims=True)
+    for copy in copies:
+        copy.wait()
 
 
 def body(radiances, band, row_in_band, column):
@@ -280,20 +355,31 @@
     cap = 2 * obs // nrows
     nfeat = 1 + 4 * fields
     vmem = pl.BlockSpec(memory_space=pltpu.VMEM)
+    anywhere = pl.BlockSpec(memory_space=pl.ANY)
     dma = pltpu.SemaphoreType.DMA
-    return pl.pallas_call(
+    band = band.reshape(1, obs)
+    shapes = (
+        ((ROWS_DEV, COLS), jnp.int32),
+        ((fields, ROWS_DEV, COLS), F32),
+        ((fields, ROWS_DEV, COLS), F32),
+        ((ROWS_DEV, COLS), F32),
+    )
+    held = pl.pallas_call(
         functools.partial(kernel, nrows, nchan),
-        out_shape=(
-            jax.ShapeDtypeStruct((ROWS_DEV, COLS), jnp.int32),
-            jax.ShapeDtypeStruct((fields, ROWS_DEV, COLS), F32),
-            jax.ShapeDtypeStruct((fields, ROWS_DEV, COLS), F32),
-            jax.ShapeDtypeStruct((ROWS_DEV, COLS), F32),
-            jax.ShapeDtypeStruct((fields, obs), F32),
+        out_shape=tuple(pltpu.VMEM(s, t) for s, t in shapes)
+        + (
+            pltpu.VMEM((fields, obs), F32),
+            pltpu.VMEM((nrows, cap), F32),
+            pltpu.VMEM((cap, obs), BF16),
+            pltpu.VMEM((1, obs), jnp.int32),
         ),
-        in_specs=[vmem] * 4,
-        out_specs=(vmem,) * 5,
+        in_specs=[pl.BlockSpec(memory_space=pltpu.HBM)] * 4,
+        out_specs=(vmem,) * 8,
         scratch_shapes=[
-            pltpu.VMEM((cap, obs), BF16),
+            pltpu.VMEM((fields, obs), F32),
+            pltpu.VMEM((1, obs), jnp.int32),
+            pltpu.VMEM((1, obs), jnp.int32),
+            pltpu.VMEM((1, obs), jnp.int32),
             pltpu.VMEM((nrows, LOW, cap), BF16),
             pltpu.VMEM((nrows, QS, cap), F32),
             pltpu.VMEM((nfeat * QS, LOW), F32),
@@ -304,6 +390,9 @@
             pltpu.VMEM((nchan, QS, LOW), F32),
             pltpu.VMEM((nrows, fields, cap), F32),
             pltpu.VMEM((nrows, fields, cap), F32),
+            pltpu.VMEM((nrows, 1, cap), F32),
+            pltpu.VMEM((nrows, 1, cap), F32),
+            dma((4,)),
             dma((nrows,)),
             dma((nrows,)),
             dma((nrows,)),
@@ -312,14 +401,27 @@
             dma((nchan,)),
             dma((nrows,)),
             dma((nrows,)),
+            dma((nrows,)),
+            dma((nrows,)),
         ],
-        compiler_params=pltpu.CompilerParams(collective_id=0, has_side_effects=True),
+        compiler_params=pltpu.CompilerParams(
+            collective_id=0, has_side_effects=True, vmem_limit_bytes=32 * 1024 * 1024
+        ),
     )(
-        radiances,
-        band.reshape(1, obs),
-        row_in_band.reshape(1, obs),
-        column.reshape(1, obs),
+        *(
+            pltpu.with_memory_space_constraint(x, pltpu.HBM)
+            for x in (radiances, band, row_in_band.reshape(1, obs), column.reshape(1, obs))
+        )
     )
+    return pl.pallas_call(
+        functools.partial(finish, nrows),
+        out_shape=tuple(jax.ShapeDtypeStruct(s, t) for s, t in shapes)
+        + (jax.ShapeDtypeStruct((fields, obs), F32),),
+        in_specs=[vmem] * 8,
+        out_specs=(anywhere,) * 4 + (vmem,),
+        scratch_shapes=[dma((4,))],
+        compiler_params=pltpu.CompilerParams(vmem_limit_bytes=32 * 1024 * 1024),
+    )(*held)
 
 
 def solution(mesh):

time: 27.8 us -> 21.8 us (0.78)
  local copies, waits for them, and re-layouts: 5.04 us -> 0 us
  Pallas kernels: 21.7 us -> 21 us
    unnamed x11 -> x0, local copies, waits for them, and re-layouts: 5.04 us -> none
    pallas_call x1 -> x2, Pallas kernels: 21.7 us -> 21 us  [the longest x1 19.6 us: body(): pl.pallas_call(functools.partial(kernel, nrows, nchan), out_shape=tuple((...]
where the time goes in v2:
time: 21.8 us; the launch traced here: 21.6 us
  Pallas kernels  21 us (96%)
  between operations  0.64 us (3%)
    pallas_call x1, Pallas kernels, body(): pl.pallas_call(functools.partial(kernel, nrows, nchan), out_shape=tuple((...  19.6 us
    pallas_call x1, Pallas kernels, body(): pl.pallas_call(functools.partial(finish, nrows), out_shape=tuple((jax.Sha...  1.37 us

profile of v2, /device:TPU:0, one launch (start us, length us, event | category | flops | bytes accessed | tf_op | source)
XLA Modules:
  0.0 21.6 jit_solution(1511423135117678871)
XLA Ops:
  0.6 19.6 %shard_map.83 = (s32[4,1440]{1,0:T(4,128)S(1)}, f32[4,4,1440]{2,1,0:T(4,128)S(1)}, f32[4,4,1440]{2,1,0:T(4,128)S(1)}, f32[4,1440]{1,0:T(4,128)S(1)}, f32[4,2048]...) custom-call(f32[4,2048]{1,0:T(4,128)} %rad_in.1, ...), custom_call_target="tpu_custom_call" | custom-call | tf_op jit(solution)/shard_map/pallas_call | solution.py:367
  20.2 1.4 %shard_map.84 = (s32[4,1440]{1,0:T(4,128)}, f32[4,4,1440]{2,1,0:T(4,128)}, f32[4,4,1440]{2,1,0:T(4,128)}, f32[4,1440]{1,0:T(4,128)}, f32[4,2048]{1,0:T(4,128)}) custom-call(s32[4,1440]{1,0:T(4,128)S(1)} %get-tuple-element.13.cnt_ref, f32[4,4,1440]{2,1,0:T(4,128)S(1)} %get-tuple-element.14.mean_ref, f32[4,4,1440]{2,1,0:T(4,128)S(1)} %get-tuple-element.15.var_ref, ...), custom_call_target="tpu_custom_call" | custom-call | tf_op jit(solution)/shard_map/pallas_call | solution.py:416

commit v3 on v2

--- a/solution.py
+++ b/solution.py
@@ -142,14 +142,11 @@
     for fetch in fetches:
         fetch.start()
     barrier = pltpu.get_barrier_semaphore()
-    for d in range(1, nrows):
-        pl.semaphore_signal(
-            barrier, inc=1, device_id={"rows": lax.rem(me + d, nrows)}, device_id_type=MESH
-        )
-    for d in range(1, nchan):
-        pl.semaphore_signal(
-            barrier, inc=1, device_id={"chan": lax.rem(mc + d, nchan)}, device_id_type=MESH
-        )
+    for d in range(nrows):
+        for e in range(nchan):
+            if d + e > 0:
+                to = {"rows": lax.rem(me + d, nrows), "chan": lax.rem(mc + e, nchan)}
+                pl.semaphore_signal(barrier, inc=1, device_id=to, device_id_type=MESH)
 
     fetches[0].wait()
     dest = band_ref[...]
@@ -173,7 +170,7 @@
         [jnp.where(dest == lax.rem(me + d, nrows), payload, 0.0) for d in range(nrows)], axis=0
     ).astype(BF16)
     placed = dot(left, rank_hot[...], NT)
-    pl.semaphore_wait(barrier, nrows - 1 + nchan - 1)
+    pl.semaphore_wait(barrier, nrows * nchan - 1)
 
     out_copies = []
     for d in list(range(1, nrows)) + [0]:
@@ -233,20 +230,31 @@
     partial = variances[0]
     for f in range(1, fields):
         partial = partial + variances[f]
-    parts[mc] = partial
-    part_copies = []
-    for d in range(1, nchan):
-        copy = pltpu.make_async_remote_copy(
-            src_ref=parts.at[mc],
-            dst_ref=parts.at[mc],
-            send_sem=sp.at[d],
-            recv_sem=rp.at[d],
-            device_id={"chan": lax.rem(mc + d, nchan)},
-            device_id_type=MESH,
-        )
-        copy.start()
-        part_copies.append(copy)
-
+    table = jnp.concatenate(two(partial), axis=0).astype(BF16)
+    scale_copies = []
+    for d in list(range(1, nrows)) + [0]:
+        picked = dot(table, col_hot[d], NN)
+        found = jnp.sum((picked[:QS] + picked[QS:]) * q_hot[d], axis=0, keepdims=True)
+        scale_s[d] = found
+        if d == 0:
+            scale_r[0] = found
+        for e in range(nchan):
+            if d + e == 0:
+                continue
+            slot = e * nrows + d
+            copy = pltpu.make_async_remote_copy(
+                src_ref=scale_s.at[d],
+                dst_ref=scale_r.at[slot],
+                send_sem=ss.at[slot],
+                recv_sem=rs.at[slot],
+                device_id={
+                    "rows": lax.rem(me + nrows - d, nrows),
+                    "chan": lax.rem(mc + e, nchan),
+                },
+                device_id_type=MESH,
+            )
+            copy.start()
+            scale_copies.append(copy)
     split = [two(mean) for mean in means]
     table = jnp.concatenate([x[0] for x in split] + [x[1] for x in split], axis=0).astype(BF16)
     back_copies = []
@@ -274,44 +282,42 @@
         copy.start()
         back_copies.append(copy)
 
+    parts[mc] = partial
+    part_copies = []
+    for d in range(1, nchan):
+        copy = pltpu.make_async_remote_copy(
+            src_ref=parts.at[mc],
+            dst_ref=parts.at[mc],
+            send_sem=sp.at[d],
+            recv_sem=rp.at[d],
+            device_id={"chan": lax.rem(mc + d, nchan)},
+            device_id_type=MESH,
+        )
+        copy.start()
+        part_copies.append(copy)
+
+    spill(cnt_out, count)
+    for f in range(fields):
+        spill(mean_out.at[f], means[f])
+        spill(var_out.at[f], variances[f])
+
+    for copy in back_copies:
+        copy.wait_recv()
+    returned = jnp.concatenate([back_r[d] for d in range(nrows)], axis=0)
+    diff_out[...] = unplace(me, nrows, fields, returned, rank_hot, dest)
     for copy in part_copies:
         copy.wait_recv()
     spread = parts[0]
     for c in range(1, nchan):
         spread = spread + parts[c]
-    scale = lax.rsqrt(1.0 + spread / CHAN)
-    table = jnp.concatenate(two(scale), axis=0).astype(BF16)
-    scale_copies = []
-    for d in list(range(1, nrows)) + [0]:
-        picked = dot(table, col_hot[d], NN)
-        found = jnp.sum((picked[:QS] + picked[QS:]) * q_hot[d], axis=0, keepdims=True)
-        if d == 0:
-            scale_r[0] = found
-            continue
-        scale_s[d] = found
-        copy = pltpu.make_async_remote_copy(
-            src_ref=scale_s.at[d],
-            dst_ref=scale_r.at[d],
-            send_sem=ss.at[d],
-            recv_sem=rs.at[d],
-            device_id={"rows": lax.rem(me + nrows - d, nrows)},
-            device_id_type=MESH,
-        )
-        copy.start()
-        scale_copies.append(copy)
     spill(spr_out, spread)
-    spill(cnt_out, count)
-    for f in range(fields):
-        spill(mean_out.at[f], means[f])
-        spill(var_out.at[f], variances[f])
-
-    for copy in back_copies:
-        copy.wait_recv()
-    returned = jnp.concatenate([back_r[d] for d in range(nrows)], axis=0)
-    diff_out[...] = unplace(me, nrows, fields, returned, rank_hot, dest)
     for copy in scale_copies:
         copy.wait_recv()
-    scale_out[...] = jnp.concatenate([scale_r[d] for d in range(nrows)], axis=0)
+    spreads = None
+    for e in range(nchan):
+        rows = jnp.concatenate([scale_r[e * nrows + d] for d in range(nrows)], axis=0)
+        spreads = rows if spreads is None else spreads + rows
+    scale_out[...] = lax.rsqrt(1.0 + spreads / CHAN)
 
     for copy in out_copies + part_copies + back_copies + scale_copies:
         copy.wait_send()
@@ -391,7 +397,7 @@
             pltpu.VMEM((nrows, fields, cap), F32),
             pltpu.VMEM((nrows, fields, cap), F32),
             pltpu.VMEM((nrows, 1, cap), F32),
-            pltpu.VMEM((nrows, 1, cap), F32),
+            pltpu.VMEM((nchan * nrows, 1, cap), F32),
             dma((4,)),
             dma((nrows,)),
             dma((nrows,)),
@@ -401,8 +407,8 @@
             dma((nchan,)),
             dma((nrows,)),
             dma((nrows,)),
-            dma((nrows,)),
-            dma((nrows,)),
+            dma((nchan * nrows,)),
+            dma((nchan * nrows,)),
         ],
         compiler_params=pltpu.CompilerParams(
             collective_id=0, has_side_effects=True, vmem_limit_bytes=32 * 1024 * 1024

time: 21.8 us -> 21.6 us (level)
  no operation moved by 1% of the time
where the time goes in v3:
time: 21.6 us; the launch traced here: 21.4 us
  Pallas kernels  20.8 us (96%)
  between operations  0.64 us (3%)
    pallas_call x1, Pallas kernels, body(): pl.pallas_call(functools.partial(kernel, nrows, nchan), out_shape=tuple((...  19.4 us
    pallas_call x1, Pallas kernels, body(): pl.pallas_call(functools.partial(finish, nrows), out_shape=tuple((jax.Sha...  1.37 us

profile of v3, /device:TPU:0, one launch (start us, length us, event | category | flops | bytes accessed | tf_op | source)
XLA Modules:
  0.0 21.4 jit_solution(3797324907654337186)
XLA Ops:
  0.6 19.4 %shard_map.83 = (s32[4,1440]{1,0:T(4,128)S(1)}, f32[4,4,1440]{2,1,0:T(4,128)S(1)}, f32[4,4,1440]{2,1,0:T(4,128)S(1)}, f32[4,1440]{1,0:T(4,128)S(1)}, f32[4,2048]...) custom-call(f32[4,2048]{1,0:T(4,128)} %rad_in.1, ...), custom_call_target="tpu_custom_call" | custom-call | tf_op jit(solution)/shard_map/pallas_call | solution.py:373
  20.0 1.4 %shard_map.84 = (s32[4,1440]{1,0:T(4,128)}, f32[4,4,1440]{2,1,0:T(4,128)}, f32[4,4,1440]{2,1,0:T(4,128)}, f32[4,1440]{1,0:T(4,128)}, f32[4,2048]{1,0:T(4,128)}) custom-call(s32[4,1440]{1,0:T(4,128)S(1)} %get-tuple-element.13.cnt_ref, f32[4,4,1440]{2,1,0:T(4,128)S(1)} %get-tuple-element.14.mean_ref, f32[4,4,1440]{2,1,0:T(4,128)S(1)} %get-tuple-element.15.var_ref, ...), custom_call_target="tpu_custom_call" | custom-call | tf_op jit(solution)/shard_map/pallas_call | solution.py:422

commit v4 on v3

--- a/solution.py
+++ b/solution.py
@@ -11,6 +11,7 @@
 COLS = 1440
 ROWS_DEV = 4
 LOW = 256
+LANES = 128
 BLOCKS = -(-COLS // LOW)
 QS = BLOCKS * ROWS_DEV
 F32 = jnp.float32
@@ -65,26 +66,6 @@
         )
 
 
-def unplace(me, nrows, fields, returned, rank_hot, dest):
-    size = nrows * fields
-    both = dot(jnp.concatenate(two(returned), axis=0).astype(BF16), rank_hot[...], NN)
-    merged = both[:size] + both[size:]
-    per = max(1, 8 // fields)
-    inside = jnp.zeros((per * fields, 1), jnp.int32)
-    for j in range(1, per):
-        inside = inside + (iota((per * fields, 1), 0) >= j * fields).astype(jnp.int32)
-    result = None
-    for p in range(nrows // per):
-        owner = lax.rem(me + p * per + inside, nrows)
-        block = merged[p * per * fields : (p + 1) * per * fields]
-        term = jnp.where(dest == owner, block, 0.0)
-        result = term if result is None else result + term
-    final = result[:fields]
-    for j in range(1, per):
-        final = final + result[j * fields : (j + 1) * fields]
-    return final
-
-
 def kernel(
     nrows,
     nchan,
@@ -98,8 +79,9 @@
     spr_out,
     diff_out,
     scale_out,
+    rank_out,
+    dest_out,
     rank_hot,
-    dest_out,
     rad_ref,
     band_ref,
     rib_ref,
@@ -152,6 +134,7 @@
     dest = band_ref[...]
     dest_out[...] = dest
     rank = rank_of(dest, nrows)
+    rank_out[...] = rank
     rank_hot[...] = onehot(iota((cap, obs), 0) == rank).astype(BF16)
     for fetch in fetches[1:]:
         fetch.wait()
@@ -230,6 +213,33 @@
     partial = variances[0]
     for f in range(1, fields):
         partial = partial + variances[f]
+    split = [two(mean) for mean in means]
+    table = jnp.concatenate([x[0] for x in split] + [x[1] for x in split], axis=0).astype(BF16)
+    back_copies = []
+    for d in list(range(1, nrows)) + [0]:
+        picked = dot(table, col_hot[d], NN)
+        quads = q_hot[d]
+        found = []
+        for f in range(fields):
+            at = (fields + f) * QS
+            both = picked[f * QS : (f + 1) * QS] + picked[at : at + QS]
+            found.append(jnp.sum(both * quads, axis=0, keepdims=True))
+        diff = recv_v[d] - jnp.concatenate(found, axis=0)
+        if d == 0:
+            back_r[0] = diff
+            continue
+        back_s[d] = diff
+        copy = pltpu.make_async_remote_copy(
+            src_ref=back_s.at[d],
+            dst_ref=back_r.at[d],
+            send_sem=sb.at[d],
+            recv_sem=rb.at[d],
+            device_id={"rows": lax.rem(me + nrows - d, nrows)},
+            device_id_type=MESH,
+        )
+        copy.start()
+        back_copies.append(copy)
+
     table = jnp.concatenate(two(partial), axis=0).astype(BF16)
     scale_copies = []
     for d in list(range(1, nrows)) + [0]:
@@ -255,33 +265,6 @@
             )
             copy.start()
             scale_copies.append(copy)
-    split = [two(mean) for mean in means]
-    table = jnp.concatenate([x[0] for x in split] + [x[1] for x in split], axis=0).astype(BF16)
-    back_copies = []
-    for d in list(range(1, nrows)) + [0]:
-        picked = dot(table, col_hot[d], NN)
-        quads = q_hot[d]
-        found = []
-        for f in range(fields):
-            at = (fields + f) * QS
-            both = picked[f * QS : (f + 1) * QS] + picked[at : at + QS]
-            found.append(jnp.sum(both * quads, axis=0, keepdims=True))
-        diff = recv_v[d] - jnp.concatenate(found, axis=0)
-        if d == 0:
-            back_r[0] = diff
-            continue
-        back_s[d] = diff
-        copy = pltpu.make_async_remote_copy(
-            src_ref=back_s.at[d],
-            dst_ref=back_r.at[d],
-            send_sem=sb.at[d],
-            recv_sem=rb.at[d],
-            device_id={"rows": lax.rem(me + nrows - d, nrows)},
-            device_id_type=MESH,
-        )
-        copy.start()
-        back_copies.append(copy)
-
     parts[mc] = partial
     part_copies = []
     for d in range(1, nchan):
@@ -303,8 +286,7 @@
 
     for copy in back_copies:
         copy.wait_recv()
-    returned = jnp.concatenate([back_r[d] for d in range(nrows)], axis=0)
-    diff_out[...] = unplace(me, nrows, fields, returned, rank_hot, dest)
+    diff_out[...] = back_r[...]
     for copy in part_copies:
         copy.wait_recv()
     spread = parts[0]
@@ -331,8 +313,8 @@
     spr_ref,
     diff_ref,
     scale_ref,
-    rank_hot,
-    band_ref,
+    rank_ref,
+    dest_ref,
     cnt_out,
     mean_out,
     var_out,
@@ -345,11 +327,35 @@
     for copy in copies:
         copy.start()
     me = lax.axis_index("rows")
-    both = dot(jnp.concatenate(two(scale_ref[...]), axis=0).astype(BF16), rank_hot[...], NN)
-    merged = both[:nrows] + both[nrows:]
-    owner = lax.rem(me + iota((nrows, 1), 0), nrows)
-    mine = jnp.where(band_ref[...] == owner, merged, 0.0)
-    dep_out[...] = diff_ref[...] * jnp.sum(mine, axis=0, keepdims=True)
+    fields, obs = dep_out.shape
+    tiles = -(-scale_ref.shape[1] // LANES)
+    lines = obs // LANES
+
+    def folded(ref):
+        return jnp.concatenate(
+            [ref[:, k * LANES : (k + 1) * LANES] for k in range(lines)], axis=0
+        )
+
+    rank = folded(rank_ref)
+    distance = lax.rem(folded(dest_ref) - me + nrows, nrows)
+    place = distance * tiles + rank // LANES
+    lane = rank & (LANES - 1)
+    found = [jnp.zeros((lines, LANES), F32) for _ in range(fields + 1)]
+    for d in range(nrows):
+        for t in range(tiles):
+            here = place == d * tiles + t
+            span = slice(t * LANES, (t + 1) * LANES)
+            for f in range(fields + 1):
+                row = scale_ref[d : d + 1, span] if f == fields else diff_ref[d, f : f + 1, span]
+                taken = jnp.take_along_axis(
+                    jnp.broadcast_to(row, (lines, LANES)), lane, axis=1, mode="promise_in_bounds"
+                )
+                found[f] = jnp.where(here, taken, found[f])
+    results = [found[f] * found[fields] for f in range(fields)]
+    for k in range(lines):
+        dep_out[:, k * LANES : (k + 1) * LANES] = jnp.concatenate(
+            [x[k : k + 1] for x in results], axis=0
+        )
     for copy in copies:
         copy.wait()
 
@@ -374,14 +380,15 @@
         functools.partial(kernel, nrows, nchan),
         out_shape=tuple(pltpu.VMEM(s, t) for s, t in shapes)
         + (
-            pltpu.VMEM((fields, obs), F32),
+            pltpu.VMEM((nrows, fields, cap), F32),
             pltpu.VMEM((nrows, cap), F32),
-            pltpu.VMEM((cap, obs), BF16),
+            pltpu.VMEM((1, obs), jnp.int32),
             pltpu.VMEM((1, obs), jnp.int32),
         ),
         in_specs=[pl.BlockSpec(memory_space=pltpu.HBM)] * 4,
         out_specs=(vmem,) * 8,
         scratch_shapes=[
+            pltpu.VMEM((cap, obs), BF16),
             pltpu.VMEM((fields, obs), F32),
             pltpu.VMEM((1, obs), jnp.int32),
             pltpu.VMEM((1, obs), jnp.int32),

time: 21.6 us -> 21 us (0.972)
  Pallas kernels: 20.8 us -> 20.1 us
    pallas_call x1, Pallas kernels: 19.4 us -> 18.7 us  [body(): pl.pallas_call(functools.partial(kernel, nrows, nchan), out_shape=tuple((...]
where the time goes in v4:
time: 21 us; the launch traced here: 20.7 us
  Pallas kernels  20.1 us (96%)
  between operations  0.64 us (3%)
    pallas_call x1, Pallas kernels, body(): pl.pallas_call(functools.partial(kernel, nrows, nchan), out_shape=tuple((...  18.7 us
    pallas_call x1, Pallas kernels, body(): pl.pallas_call(functools.partial(finish, nrows), out_shape=tuple((jax.Sha...  1.38 us

profile of v4, /device:TPU:0, one launch (start us, length us, event | category | flops | bytes accessed | tf_op | source)
XLA Modules:
  0.0 20.7 jit_solution(4108327758529675880)
XLA Ops:
  0.6 18.7 %shard_map.83 = (s32[4,1440]{1,0:T(4,128)S(1)}, f32[4,4,1440]{2,1,0:T(4,128)S(1)}, f32[4,4,1440]{2,1,0:T(4,128)S(1)}, f32[4,1440]{1,0:T(4,128)S(1)}, f32[8,4,512...) custom-call(f32[4,2048]{1,0:T(4,128)} %rad_in.1, s32[1,2048]{1,0:T(1,128)} %bitcast.3, ...), custom_call_target="tpu_custom_call" | custom-call | tf_op jit(solution)/shard_map/pallas_call | solution.py:379
  19.4 1.4 %shard_map.84 = (s32[4,1440]{1,0:T(4,128)}, f32[4,4,1440]{2,1,0:T(4,128)}, f32[4,4,1440]{2,1,0:T(4,128)}, f32[4,1440]{1,0:T(4,128)}, f32[4,2048]{1,0:T(4,128)}) custom-call(s32[4,1440]{1,0:T(4,128)S(1)} %get-tuple-element.13.cnt_ref, f32[4,4,1440]{2,1,0:T(4,128)S(1)} %get-tuple-element.14.mean_ref, f32[4,4,1440]{2,1,0:T(4,128)S(1)} %get-tuple-element.15.var_ref, ...), custom_call_target="tpu_custom_call" | custom-call | tf_op jit(solution)/shard_map/pallas_call | solution.py:429

commit v5 on v4

--- a/solution.py
+++ b/solution.py
@@ -214,40 +214,35 @@
     for f in range(1, fields):
         partial = partial + variances[f]
     split = [two(mean) for mean in means]
+    split.append(two(partial))
     table = jnp.concatenate([x[0] for x in split] + [x[1] for x in split], axis=0).astype(BF16)
     back_copies = []
+    scale_copies = []
     for d in list(range(1, nrows)) + [0]:
         picked = dot(table, col_hot[d], NN)
         quads = q_hot[d]
         found = []
-        for f in range(fields):
-            at = (fields + f) * QS
+        for f in range(fields + 1):
+            at = (fields + 1 + f) * QS
             both = picked[f * QS : (f + 1) * QS] + picked[at : at + QS]
             found.append(jnp.sum(both * quads, axis=0, keepdims=True))
-        diff = recv_v[d] - jnp.concatenate(found, axis=0)
+        diff = recv_v[d] - jnp.concatenate(found[:fields], axis=0)
+        scale_s[d] = found[fields]
         if d == 0:
             back_r[0] = diff
-            continue
-        back_s[d] = diff
-        copy = pltpu.make_async_remote_copy(
-            src_ref=back_s.at[d],
-            dst_ref=back_r.at[d],
-            send_sem=sb.at[d],
-            recv_sem=rb.at[d],
-            device_id={"rows": lax.rem(me + nrows - d, nrows)},
-            device_id_type=MESH,
-        )
-        copy.start()
-        back_copies.append(copy)
-
-    table = jnp.concatenate(two(partial), axis=0).astype(BF16)
-    scale_copies = []
-    for d in list(range(1, nrows)) + [0]:
-        picked = dot(table, col_hot[d], NN)
-        found = jnp.sum((picked[:QS] + picked[QS:]) * q_hot[d], axis=0, keepdims=True)
-        scale_s[d] = found
-        if d == 0:
-            scale_r[0] = found
+            scale_r[0] = found[fields]
+        if d > 0:
+            back_s[d] = diff
+            copy = pltpu.make_async_remote_copy(
+                src_ref=back_s.at[d],
+                dst_ref=back_r.at[d],
+                send_sem=sb.at[d],
+                recv_sem=rb.at[d],
+                device_id={"rows": lax.rem(me + nrows - d, nrows)},
+                device_id_type=MESH,
+            )
+            copy.start()
+            back_copies.append(copy)
         for e in range(nchan):
             if d + e == 0:
                 continue
@@ -265,6 +260,7 @@
             )
             copy.start()
             scale_copies.append(copy)
+
     parts[mc] = partial
     part_copies = []
     for d in range(1, nchan):

time: 21 us -> 20.9 us (level)
  no operation moved by 1% of the time
where the time goes in v5:
time: 20.9 us; the launch traced here: 20.6 us
  Pallas kernels  20 us (96%)
  between operations  0.64 us (3%)
    pallas_call x1, Pallas kernels, body(): pl.pallas_call(functools.partial(kernel, nrows, nchan), out_shape=tuple((...  18.6 us
    pallas_call x1, Pallas kernels, body(): pl.pallas_call(functools.partial(finish, nrows), out_shape=tuple((jax.Sha...  1.38 us

profile of v5, /device:TPU:0, one launch (start us, length us, event | category | flops | bytes accessed | tf_op | source)
XLA Modules:
  0.0 20.6 jit_solution(12360498321408272429)
XLA Ops:
  0.6 18.6 %shard_map.83 = (s32[4,1440]{1,0:T(4,128)S(1)}, f32[4,4,1440]{2,1,0:T(4,128)S(1)}, f32[4,4,1440]{2,1,0:T(4,128)S(1)}, f32[4,1440]{1,0:T(4,128)S(1)}, f32[8,4,512...) custom-call(f32[4,2048]{1,0:T(4,128)} %rad_in.1, s32[1,2048]{1,0:T(1,128)} %bitcast.3, ...), custom_call_target="tpu_custom_call" | custom-call | tf_op jit(solution)/shard_map/pallas_call | solution.py:375
  19.3 1.4 %shard_map.84 = (s32[4,1440]{1,0:T(4,128)}, f32[4,4,1440]{2,1,0:T(4,128)}, f32[4,4,1440]{2,1,0:T(4,128)}, f32[4,1440]{1,0:T(4,128)}, f32[4,2048]{1,0:T(4,128)}) custom-call(s32[4,1440]{1,0:T(4,128)S(1)} %get-tuple-element.13.cnt_ref, f32[4,4,1440]{2,1,0:T(4,128)S(1)} %get-tuple-element.14.mean_ref, f32[4,4,1440]{2,1,0:T(4,128)S(1)} %get-tuple-element.15.var_ref, ...), custom_call_target="tpu_custom_call" | custom-call | tf_op jit(solution)/shard_map/pallas_call | solution.py:425
